TPU v7x, 32 devices: a whole 2x2x4 slice. The times are simulated.
32 devices in a mesh: wide: 8 (over y, x, core), narrow: 4 (over z).
Axes of the slice: x: 2, y: 2, z: 4, core: 2. Of those that a mesh axis runs over, the one named last changes fastest.
Arguments:
- tokens: float32 [4488, 768], P('wide'), may hold values from -6 to 6
- region: int32 [4488], P('wide'), may hold values from 0 to 59, as said below
- order_rank: int32 [4488], P('wide'), may hold values from 0 to 559, as said below
- box_coords: int32 [2, 4488], P(None, 'wide'), may hold values from 0 to 127
- w_query: float32 [768, 768], P(None, 'narrow'), may hold values from -0.21875 to 0.21875
- b_query: float32 [768], P('narrow'), may hold values from -3 to 3
- w_key: float32 [768, 768], P(None, 'narrow'), may hold values from -0.21875 to 0.21875
- w_value: float32 [768, 768], P(None, 'narrow'), may hold values from -0.21875 to 0.21875
- b_value: float32 [768], P('narrow'), may hold values from -0.18 to 0.18
- w_out: float32 [768, 768], P('narrow'), may hold values from -2 to 2
- b_out: float32 [768], replicated, may hold values from -2 to 2
- ln1_gain: float32 [768], replicated, may hold values from 0.1 to 1.9
- ln1_bias: float32 [768], replicated, may hold values from -2 to 2
- w_in: float32 [768, 3072], P(None, 'narrow'), may hold values from -0.21875 to 0.21875
- b_in: float32 [3072], P('narrow'), may hold values from -2 to 2
- w_down: float32 [3072, 768], P('narrow'), may hold values from -0.109375 to 0.109375
- b_down: float32 [768], replicated, may hold values from -2 to 2
- ln2_gain: float32 [768], replicated, may hold values from 0.1 to 1.9
- ln2_bias: float32 [768], replicated, may hold values from -2 to 2
- rel_order: float32 [12, 32], P('narrow'), may hold values from -3 to 3
- rel_x: float32 [12, 64], P('narrow'), may hold values from -3 to 3
- rel_y: float32 [12, 64], P('narrow'), may hold values from -3 to 3
- cotangent: float32 [4488, 768], P('wide'), may hold values from -6 to 6
Outputs:
- output: float32 [4488, 768], P('wide')
- grad_input: float32 [4488, 768], P('wide')
- grad_w_query: float32 [768, 768], P(None, 'narrow')
- grad_b_query: float32 [768], P('narrow')
- grad_w_key: float32 [768, 768], P(None, 'narrow')
- grad_w_value: float32 [768, 768], P(None, 'narrow')
- grad_b_value: float32 [768], P('narrow')
- grad_w_out: float32 [768, 768], P('narrow')
- grad_b_out: float32 [768], replicated
- grad_ln1_gain: float32 [768], replicated
- grad_ln1_bias: float32 [768], replicated
- grad_w_in: float32 [768, 3072], P(None, 'narrow')
- grad_b_in: float32 [3072], P('narrow')
- grad_w_down: float32 [3072, 768], P('narrow')
- grad_b_down: float32 [768], replicated
- grad_ln2_gain: float32 [768], replicated
- grad_ln2_bias: float32 [768], replicated
- grad_rel_order: float32 [12, 32], P('narrow')
- grad_rel_x: float32 [12, 64], P('narrow')
- grad_rel_y: float32 [12, 64], P('narrow')
Inputs may be any that keep to these rules, and one draw needn't show every extreme that they name: Each page's region ids take every value from 0 to its region count minus 1; region counts run from 2 to min(60, 561), and one page has the most. `order_rank`: within each region of a page the ranks are 0, 1, and so on up to its size minus 1, each once; no region holds more than 560 tokens, and one page has a region of exactly 560 tokens.
All inputs are finite; a program needn't handle non-finite values.
Results may differ from a plain program's by a relative error of at most 0.015.
The roundings to bfloat16 on the way count: a program that leaves them out, or rounds other values in their place, can miss the bound.
Values sent between devices are 32-bit elements; how exact they have to be, the bound alone decides.
A program may use at most 128 MiB of HBM per device.

v0:
```python
import math
import jax
import jax.numpy as jnp
from jax import lax
from jax.sharding import PartitionSpec as P

HEAD_DIM = 64
BINS1 = 32
BINS2 = 64
MAX_ORDER = 128
MAX_LAYOUT = 256
PAGE = 561
HIGHEST = lax.Precision.HIGHEST
EPSILON = 1e-05
SCORE_SCALE = 0.125


def bucket_steps(bins, reach):
    halfway = bins // 2
    exact = halfway // 2
    steps = []
    for level in range(1, halfway):
        if level < exact:
            steps.append(level)
        else:
            found = reach + 1
            for count in range(exact, reach + 2):
                value = exact + int(
                    math.log(count / exact) / math.log(reach / exact) * (halfway - exact)
                )
                if min(value, halfway - 1) >= level:
                    found = count
                    break
            steps.append(found)
    return steps


def bucket_of(offset_grid, bins, reach):
    halfway = bins // 2
    magnitude = jnp.abs(offset_grid)
    result = jnp.where(offset_grid > 0, halfway, 0).astype(jnp.int32)
    for level_start in bucket_steps(bins, reach):
        result = result + (magnitude >= level_start).astype(jnp.int32)
    return result


def norm_layer(values, gain_row, shift_row):
    average = jnp.mean(values, axis=-1, keepdims=True)
    centred = values - average
    second = jnp.mean(centred * centred, axis=-1, keepdims=True)
    return centred * lax.rsqrt(second + EPSILON) * gain_row + shift_row


def gelu_exact(values):
    return jax.nn.gelu(values, approximate=False)


def reading_place(region, order_rank):
    earlier = (region[:, None, :] < region[:, :, None]).astype(jnp.int32)
    return (jnp.sum(earlier, axis=2) + order_rank).astype(jnp.int32)


def page_buckets(place_row, across_row, down_row):
    order_bin = bucket_of(place_row[None, :] - place_row[:, None], BINS1, MAX_ORDER)
    across_bin = bucket_of(across_row[None, :] - across_row[:, None], BINS2, MAX_LAYOUT)
    down_bin = bucket_of(down_row[None, :] - down_row[:, None], BINS2, MAX_LAYOUT)
    return (order_bin, across_bin, down_bin)


def one_hot_of(grid, bins, dtype):
    return (grid[:, :, None] == jnp.arange(bins, dtype=jnp.int32)[None, None, :]).astype(dtype)


def relative_bias(tables, read_place, across, downward):

    def relative_one_page(inputs):
        grids = page_buckets(inputs[0], inputs[1], inputs[2])
        total = None
        for table, grid in zip(tables, grids):
            chooser = one_hot_of(grid, table.shape[1], jnp.float32)
            term = jnp.einsum(
                "hb,qkb->hqk", table, chooser, precision=HIGHEST, preferred_element_type=jnp.float32
            )
            total = term if total is None else total + term
        return total

    return lax.map(relative_one_page, (read_place, across, downward))


def table_grads(grad_scores, bins_list, read_place, across, downward):

    def table_one_page(inputs):
        grad_page = inputs[0]
        grids = page_buckets(inputs[1], inputs[2], inputs[3])
        return tuple(
            (
                jnp.einsum(
                    "hqk,qkb->hb",
                    grad_page,
                    one_hot_of(grid, bins, jnp.bfloat16),
                    preferred_element_type=jnp.float32,
                )
                for grid, bins in zip(grids, bins_list)
            )
        )

    per_page = lax.map(table_one_page, (grad_scores, read_place, across, downward))
    return tuple((jnp.sum(member, axis=0) for member in per_page))


def forward(tokens, lowered, biases, rel_bias):
    query_weight, key_weight, value_weight, out_weight, in_weight, down_weight = lowered
    b_query, b_value, b_out, ln1_gain, ln1_bias, b_in, b_down, ln2_gain, ln2_bias = biases
    page_count, head_count, length = (rel_bias.shape[0], rel_bias.shape[1], rel_bias.shape[2])
    shape_heads = (page_count, length, head_count, HEAD_DIM)
    tokens_low = tokens.astype(jnp.bfloat16)
    query_rows = (
        jnp.dot(tokens_low, query_weight, preferred_element_type=jnp.float32) + b_query
    ).astype(jnp.bfloat16)
    key_rows = jnp.dot(tokens_low, key_weight, preferred_element_type=jnp.float32).astype(
        jnp.bfloat16
    )
    value_rows = (
        jnp.dot(tokens_low, value_weight, preferred_element_type=jnp.float32) + b_value
    ).astype(jnp.bfloat16)
    scores = (
        jnp.einsum(
            "pqhe,pkhe->phqk",
            query_rows.reshape(shape_heads),
            key_rows.reshape(shape_heads),
            preferred_element_type=jnp.float32,
        )
        * SCORE_SCALE
        + rel_bias
    )
    row_top = jnp.max(scores, axis=-1, keepdims=True)
    raised = jnp.exp(scores - row_top)
    row_total = jnp.sum(raised, axis=-1, keepdims=True)
    attention = raised / row_total
    log_total = row_top + jnp.log(row_total)
    mixed = jnp.einsum(
        "phqk,pkhe->pqhe",
        attention.astype(jnp.bfloat16),
        value_rows.reshape(shape_heads),
        preferred_element_type=jnp.float32,
    )
    attended = mixed.reshape(tokens.shape[0], -1).astype(jnp.bfloat16)
    partial_value = jnp.dot(attended, out_weight, preferred_element_type=jnp.float32)
    branch = lax.psum(partial_value, "narrow") + b_out
    residual_one = tokens + branch
    hidden = norm_layer(residual_one, ln1_gain, ln1_bias)
    hidden_low = hidden.astype(jnp.bfloat16)
    pre_gelu = jnp.dot(hidden_low, in_weight, preferred_element_type=jnp.float32) + b_in
    active = gelu_exact(pre_gelu).astype(jnp.bfloat16)
    ff_part = jnp.dot(active, down_weight, preferred_element_type=jnp.float32)
    residual_two = hidden + (lax.psum(ff_part, "narrow") + b_down)
    output = norm_layer(residual_two, ln2_gain, ln2_bias)
    kept_values = (
        tokens_low,
        query_rows,
        key_rows,
        value_rows,
        log_total,
        attended,
        residual_one,
        hidden_low,
        pre_gelu,
        active,
        residual_two,
    )
    return (output, kept_values)


def local(
    tokens,
    region,
    order_rank,
    box_coords,
    w_query,
    b_query,
    w_key,
    w_value,
    b_value,
    w_out,
    b_out,
    ln1_gain,
    ln1_bias,
    w_in,
    b_in,
    w_down,
    b_down,
    ln2_gain,
    ln2_bias,
    rel_order,
    rel_x,
    rel_y,
    cotangent,
):
    length = PAGE
    page_count = tokens.shape[0] // length
    read_place = reading_place(
        region.reshape(page_count, length), order_rank.reshape(page_count, length)
    )
    corners = box_coords.reshape(2, page_count, length)
    rel_bias = relative_bias((rel_order, rel_x, rel_y), read_place, corners[0], corners[1])
    lowered = tuple(
        (weight.astype(jnp.bfloat16) for weight in (w_query, w_key, w_value, w_out, w_in, w_down))
    )
    query_weight, key_weight, value_weight, out_weight, in_weight, down_weight = lowered
    biases = (b_query, b_value, b_out, ln1_gain, ln1_bias, b_in, b_down, ln2_gain, ln2_bias)
    output, kept_values = forward(tokens, lowered, biases, rel_bias)
    tokens_again = lax.optimization_barrier((tokens, output))[0]
    kept_values = forward(tokens_again, lowered, biases, rel_bias)[1]
    (
        tokens_low,
        query_rows,
        key_rows,
        value_rows,
        log_total,
        attended,
        residual_one,
        hidden_low,
        pre_gelu,
        active,
        residual_two,
    ) = kept_values
    head_count = rel_bias.shape[1]
    shape_heads = (page_count, length, head_count, HEAD_DIM)
    head_width = head_count * HEAD_DIM
    _, second_back = jax.vjp(norm_layer, residual_two, ln2_gain, ln2_bias)
    grad_residual_two, grad_ln2_gain, grad_ln2_bias = second_back(cotangent)
    grad_ff = grad_residual_two.astype(jnp.bfloat16)
    grad_b_down = jnp.sum(grad_ff, axis=0, dtype=jnp.float32)
    grad_w_down = jnp.einsum("tf,td->fd", active, grad_ff, preferred_element_type=jnp.float32)
    grad_active = jnp.einsum("td,fd->tf", grad_ff, down_weight, preferred_element_type=jnp.float32)
    _, gelu_back = jax.vjp(gelu_exact, pre_gelu)
    grad_pre = gelu_back(grad_active)[0].astype(jnp.bfloat16)
    grad_b_in = jnp.sum(grad_pre, axis=0, dtype=jnp.float32)
    grad_w_in = jnp.einsum("td,tf->df", hidden_low, grad_pre, preferred_element_type=jnp.float32)
    hidden_part = jnp.einsum("tf,df->td", grad_pre, in_weight, preferred_element_type=jnp.float32)
    grad_hidden = grad_residual_two + lax.psum(hidden_part, "narrow")
    _, first_back = jax.vjp(norm_layer, residual_one, ln1_gain, ln1_bias)
    grad_residual_one, grad_ln1_gain, grad_ln1_bias = first_back(grad_hidden)
    grad_branch = grad_residual_one.astype(jnp.bfloat16)
    grad_b_out = jnp.sum(grad_branch, axis=0, dtype=jnp.float32)
    grad_w_out = jnp.einsum("tc,td->cd", attended, grad_branch, preferred_element_type=jnp.float32)
    grad_attended = jnp.einsum(
        "td,cd->tc", grad_branch, out_weight, preferred_element_type=jnp.float32
    ).astype(jnp.bfloat16)
    query_heads = query_rows.reshape(shape_heads)
    key_heads = key_rows.reshape(shape_heads)
    value_heads = value_rows.reshape(shape_heads)
    grad_heads = grad_attended.reshape(shape_heads)
    scores = (
        jnp.einsum("pqhe,pkhe->phqk", query_heads, key_heads, preferred_element_type=jnp.float32)
        * SCORE_SCALE
        + rel_bias
    )
    attention = jnp.exp(scores - log_total)
    grad_attention = jnp.einsum(
        "pqhe,pkhe->phqk", grad_heads, value_heads, preferred_element_type=jnp.float32
    )
    inner_sum = jnp.sum(attention * grad_attention, axis=-1, keepdims=True)
    grad_scores = (attention * (grad_attention - inner_sum)).astype(jnp.bfloat16)
    grad_rel_order, grad_rel_x, grad_rel_y = table_grads(
        grad_scores, (BINS1, BINS2, BINS2), read_place, corners[0], corners[1]
    )
    grad_query = (
        (
            jnp.einsum(
                "phqk,pkhe->pqhe", grad_scores, key_heads, preferred_element_type=jnp.float32
            )
            * SCORE_SCALE
        )
        .astype(jnp.bfloat16)
        .reshape(-1, head_width)
    )
    grad_key = (
        (
            jnp.einsum(
                "phqk,pqhe->pkhe", grad_scores, query_heads, preferred_element_type=jnp.float32
            )
            * SCORE_SCALE
        )
        .astype(jnp.bfloat16)
        .reshape(-1, head_width)
    )
    grad_value = (
        jnp.einsum(
            "phqk,pqhe->pkhe",
            attention.astype(jnp.bfloat16),
            grad_heads,
            preferred_element_type=jnp.float32,
        )
        .astype(jnp.bfloat16)
        .reshape(-1, head_width)
    )
    grad_b_query = jnp.sum(grad_query, axis=0, dtype=jnp.float32)
    grad_b_value = jnp.sum(grad_value, axis=0, dtype=jnp.float32)
    grad_w_query = jnp.einsum(
        "td,tc->dc", tokens_low, grad_query, preferred_element_type=jnp.float32
    )
    grad_w_key = jnp.einsum("td,tc->dc", tokens_low, grad_key, preferred_element_type=jnp.float32)
    grad_w_value = jnp.einsum(
        "td,tc->dc", tokens_low, grad_value, preferred_element_type=jnp.float32
    )
    input_part = jnp.einsum(
        "tc,dc->td", grad_query, query_weight, preferred_element_type=jnp.float32
    )
    input_part = input_part + jnp.einsum(
        "tc,dc->td", grad_key, key_weight, preferred_element_type=jnp.float32
    )
    input_part = input_part + jnp.einsum(
        "tc,dc->td", grad_value, value_weight, preferred_element_type=jnp.float32
    )
    grad_input = grad_residual_one + lax.psum(input_part, "narrow")
    (
        grad_w_query,
        grad_b_query,
        grad_w_key,
        grad_w_value,
        grad_b_value,
        grad_w_out,
        grad_b_out,
        grad_ln1_gain,
        grad_ln1_bias,
        grad_rel_order,
        grad_rel_x,
        grad_rel_y,
        grad_w_in,
        grad_b_in,
        grad_w_down,
        grad_b_down,
        grad_ln2_gain,
        grad_ln2_bias,
    ) = lax.psum(
        (
            grad_w_query,
            grad_b_query,
            grad_w_key,
            grad_w_value,
            grad_b_value,
            grad_w_out,
            grad_b_out,
            grad_ln1_gain,
            grad_ln1_bias,
            grad_rel_order,
            grad_rel_x,
            grad_rel_y,
            grad_w_in,
            grad_b_in,
            grad_w_down,
            grad_b_down,
            grad_ln2_gain,
            grad_ln2_bias,
        ),
        "wide",
    )
    return (
        output,
        grad_input,
        grad_w_query,
        grad_b_query,
        grad_w_key,
        grad_w_value,
        grad_b_value,
        grad_w_out,
        grad_b_out,
        grad_ln1_gain,
        grad_ln1_bias,
        grad_w_in,
        grad_b_in,
        grad_w_down,
        grad_b_down,
        grad_ln2_gain,
        grad_ln2_bias,
        grad_rel_order,
        grad_rel_x,
        grad_rel_y,
    )


def solution(mesh):
    in_specs = (
        P("wide", None),
        P("wide"),
        P("wide"),
        P(None, "wide"),
        P(None, "narrow"),
        P("narrow"),
        P(None, "narrow"),
        P(None, "narrow"),
        P("narrow"),
        P("narrow", None),
        P(),
        P(),
        P(),
        P(None, "narrow"),
        P("narrow"),
        P("narrow", None),
        P(),
        P(),
        P(),
        P("narrow", None),
        P("narrow", None),
        P("narrow", None),
        P("wide", None),
    )
    out_specs = (
        P("wide", None),
        P("wide", None),
        P(None, "narrow"),
        P("narrow"),
        P(None, "narrow"),
        P(None, "narrow"),
        P("narrow"),
        P("narrow", None),
        P(),
        P(),
        P(),
        P(None, "narrow"),
        P("narrow"),
        P("narrow", None),
        P(),
        P(),
        P(),
        P("narrow", None),
        P("narrow", None),
        P("narrow", None),
    )
    return jax.shard_map(local, mesh=mesh, in_specs=in_specs, out_specs=out_specs, check_vma=False)
```

profile of v0, /device:TPU:0, one launch (start us, length us, event | category | flops | bytes accessed | tf_op | source)
XLA Modules:
  0.0 774.5 jit_solution(14613207930424786507)
XLA Ops:
  8.0 13.1 %fusion.116 = s32[561]{0:T(1024)S(1)} fusion(s32[561]{0:T(1024)} %param.24), kind=kLoop, calls=%fused_computation.185 | loop fusion | flops 943602 | bytes 4488 | tf_op jit(solution)/shard_map/reduce_sum | solution.py:60
  21.8 2.5 convert_add_fusion.2
  24.3 9.5 %convert_add_fusion = (s32[561,561]{0,1:T(8,128)S(1)}, s32[561,561]{0,1:T(8,128)S(1)}) fusion(s32[561]{0:T(1024)S(1)} %get-tuple-element.77, s32[561]{0:T(1024)S(1)} %get-tuple-element.76), kind=kLoop, calls=%fused_computation.182 | loop fusion | flops 61055736 | bytes 2522256 | tf_op jit(solution)/shard_map/while/body/eval_jaxpr/add | solution.py:43
  33.8 28.1 %fusion.2 = f32[561,561,3]{0,2,1:T(4,128)S(1)} fusion(s32[561,561]{0,1:T(8,128)S(1)} %get-tuple-element.126, f32[3,64]{1,0:T(4,128)S(1)} %copy-done), kind=kOutput, calls=%fused_computation.3 | convolution fusion | flops 745259328 | bytes 5036304 | tf_op jit(solution)/shard_map/while/body/eval_jaxpr/hb,qkb->hqk/dot_general | solution.py:81
  61.9 29.6 %fusion.4 = f32[561,561,3]{0,2,1:T(4,128)} fusion(s32[561,561]{0,1:T(8,128)S(1)} %get-tuple-element.127, f32[3,64]{1,0:T(4,128)S(1)} %copy-done.60), kind=kOutput, calls=%fused_computation.6 | convolution fusion | flops 745259328 | bytes 5036304 | tf_op jit(solution)/shard_map/while/body/eval_jaxpr/hb,qkb->hqk/dot_general | solution.py:81
  91.5 15.8 %fusion.10 = f32[561,561,3]{0,2,1:T(4,128)} fusion(s32[561,561]{0,1:T(8,128)S(1)} %convert_add_fusion.2, f32[3,32]{1,0:T(4,128)S(1)} %copy-done.61), kind=kOutput, calls=%fused_computation.13 | convolution fusion | flops 372629664 | bytes 5035920 | tf_op jit(solution)/shard_map/while/body/eval_jaxpr/hb,qkb->hqk/dot_general | solution.py:81
  108.9 5.0 copy_add_fusion
  118.7 4.9 fusion.120
  125.5 77.9 %all-reduce.10.cloned.1.call-done = f32[561,768]{1,0:T(8,128)} async-done(((f32[561,768]{1,0:T(8,128)}), f32[561,768]{1,0:T(8,128)}) %all-reduce.10.cloned.1.call-update) | async-done | bytes 1723408 | tf_op jit(solution)/shard_map/psum | solution.py:149
  205.9 8.9 %fusion.119 = f32[561,768]{1,0:T(8,128)} fusion(f32[561,768]{1,0:T(8,128)S(1)} %get-tuple-element.114, f32[768]{0:T(1024)S(1)} %copy-done.59, f32[768]{0:T(1024)S(1)} %copy-done.52, f32[768]{0:T(1024)S(1)} %copy-done.48, f32[561]{0:T(1024)S(1)} %add_rsqrt_fusion.1, f32[561]{0:T(1024)S(1)} %broadcast_multiply_fusion.3, f32[768,768]{1,0:T(8,128)} %param.38, ...), kind=kOutput, calls=%fused_computation.194 | convolution fusion | flops 1355334912 | bytes 8179080 | tf_op jit(solution)/shard_map/dot_general | solution.py:155
  214.9 74.4 %all-reduce.12.cloned.1.call-done = f32[561,768]{1,0:T(8,128)} async-done(((f32[561,768]{1,0:T(8,128)}), f32[561,768]{1,0:T(8,128)}) %all-reduce.12.cloned.1.call-update) | async-done | bytes 1723408 | tf_op jit(solution)/shard_map/psum | solution.py:156
  303.8 74.0 %all-reduce.14.cloned.1.call-done = f32[561,768]{1,0:T(8,128)} async-done(((f32[561,768]{1,0:T(8,128)}), f32[561,768]{1,0:T(8,128)}) %all-reduce.14.cloned.1.call-update) | async-done | bytes 1723408 | tf_op jit(solution)/shard_map/psum | solution.py:149
  380.1 6.0 multiply_convert_fusion.1
  389.2 74.4 %all-reduce.16.cloned.1.call-done = f32[561,768]{1,0:T(8,128)} async-done(((f32[561,768]{1,0:T(8,128)}), f32[561,768]{1,0:T(8,128)}) %all-reduce.16.cloned.1.call-update) | async-done | bytes 1723408 | tf_op jit(solution)/shard_map/psum | solution.py:156
  476.8 74.3 %all-reduce.18.cloned.1.call-done = f32[561,768]{1,0:T(8,128)} async-done(((f32[561,768]{1,0:T(8,128)}), f32[561,768]{1,0:T(8,128)}) %all-reduce.18.cloned.1.call-update) | async-done | bytes 1723408 | tf_op jit(solution)/shard_map/psum | solution.py:241
  551.2 2.6 multiply_reduce_fusion.2
  565.4 4.0 fusion.264
  569.4 2.9 fusion.248
  580.0 8.8 %fusion.131 = f32[3,32]{1,0:T(4,128)S(1)} fusion(s32[561,561]{0,1:T(8,128)} %copy-done.34, bf16[3,561,561]{1,2,0:T(8,128)(2,1)S(1)} %copy-done.8), kind=kOutput, calls=%fused_computation.207 | convolution fusion | flops 70497504 | bytes 3147594 | tf_op jit(solution)/shard_map/while/body/eval_jaxpr/hqk,qkb->hb/dot_general | solution.py:97
  588.9 14.6 %fusion.134 = f32[3,64]{1,0:T(4,128)S(1)} fusion(s32[561,561]{0,1:T(8,128)S(1)} %copy-done.38, bf16[3,561,561]{1,2,0:T(8,128)(2,1)S(1)} %copy-done.8), kind=kOutput, calls=%fused_computation.208 | convolution fusion | flops 140995008 | bytes 3147978 | tf_op jit(solution)/shard_map/while/body/eval_jaxpr/hqk,qkb->hb/dot_general | solution.py:97
  603.5 14.9 %fusion.137 = f32[3,64]{1,0:T(4,128)S(1)} fusion(s32[561,561]{0,1:T(8,128)S(1)} %copy-done.36, bf16[3,561,561]{1,2,0:T(8,128)(2,1)S(1)} %copy-done.8), kind=kOutput, calls=%fused_computation.209 | convolution fusion | flops 140995008 | bytes 3147978 | tf_op jit(solution)/shard_map/while/body/eval_jaxpr/hqk,qkb->hb/dot_general | solution.py:97
  618.4 25.3 %all-reduce = (f32[192]{0:T(256)}, f32[192]{0:T(256)}, f32[768]{0:T(1024)}, f32[768]{0:T(1024)}, f32[768]{0:T(1024)}, /*index=5*/f32[768]{0:T(1024)}, f32[768]{0...) all-reduce(f32[192]{0:T(256)S(1)} %reduce_sum.254, ...), channel_id=1, replica_groups=mesh['wide'=8,'narrow'=4] {'wide'}, use_global_device_ids=true, to_apply=%region_26.27 | all-reduce | flops 6240 | bytes 49920 | tf_op jit(solution)/shard_map/psum | solution.py:336
  643.7 3.4 add_add_fusion.7
  647.1 110.7 %all-reduce.22.cloned.1.call-done = (f32[768,192]{0,1:T(8,128)}, f32[768,192]{0,1:T(8,128)}, f32[768,192]{0,1:T(8,128)}, f32[192,768]{1,0:T(8,128)}, f32[768,768]{1,0:T(8,128)}, /*index=5*/f32[768,768]{1,0:T(8,128)}) async-done(((f32[768,192]{0,1:T(8,128)}, f32[768,192]{0,1:T(8,128)}, f32[768,192]{0,1:T(8,128)}, f32[192,768]{1,0:T(8,128)}, f32[768,768]{1,0:T(8,128)}, /*index=5*/f32[768,768]{1,0:T(8,128)}), ...) | async-done | bytes 7077904 | tf_op jit(solution)/shard_map/psum | solution.py:336
  (220 shorter events, 73.9 us)
Async XLA Ops:
  7.2 26.6 %copy-start = (f32[3,64]{1,0:T(4,128)S(1)}, f32[3,64]{1,0:T(4,128)}, u32[]{:S(2)}) copy-start(f32[3,64]{1,0:T(4,128)} %param.44) | copy-start | bytes 2308
  7.2 196.2 %all-reduce.10.cloned.1.call-start = ((), (), s32[]{:S(2)}) async-start(), calls=%async_computation | async-start | bytes 3489792 | tf_op jit(solution)/shard_map/psum | solution.py:149
  24.3 67.3 %copy-start.34 = (s32[561,561]{0,1:T(8,128)}, s32[561,561]{0,1:T(8,128)S(1)}, u32[]{:S(2)}) copy-start(s32[561,561]{0,1:T(8,128)S(1)} %convert_add_fusion.2) | copy-start | bytes 3776656
  33.8 28.1 %copy-start.35 = (s32[561,561]{0,1:T(8,128)}, s32[561,561]{0,1:T(8,128)S(1)}, u32[]{:S(2)}) copy-start(s32[561,561]{0,1:T(8,128)S(1)} %get-tuple-element.126) | copy-start | bytes 3776656
  33.8 28.1 %copy-start.37 = (s32[561,561]{0,1:T(8,128)}, s32[561,561]{0,1:T(8,128)S(1)}, u32[]{:S(2)}) copy-start(s32[561,561]{0,1:T(8,128)S(1)} %get-tuple-element.127) | copy-start | bytes 3776656
  33.8 28.1 %copy-start.60 = (f32[3,64]{1,0:T(4,128)S(1)}, f32[3,64]{1,0:T(4,128)}, u32[]{:S(2)}) copy-start(f32[3,64]{1,0:T(4,128)} %param.43) | copy-start | bytes 2308
  61.9 29.6 %copy-start.61 = (f32[3,32]{1,0:T(4,128)S(1)}, f32[3,32]{1,0:T(4,128)}, u32[]{:S(2)}) copy-start(f32[3,32]{1,0:T(4,128)} %param.42) | copy-start | bytes 1156
  91.5 15.8 %copy-start.3 = (f32[561,768]{1,0:T(8,128)S(1)}, f32[561,768]{1,0:T(8,128)}, u32[]{:S(2)}) copy-start(f32[561,768]{1,0:T(8,128)} %param.23) | copy-start | bytes 5170180
  91.5 15.8 %copy-start.15 = (f32[768,192]{0,1:T(8,128)S(1)}, f32[768,192]{0,1:T(8,128)}, u32[]{:S(2)}) copy-start(f32[768,192]{0,1:T(8,128)} %param.29) | copy-start | bytes 1769476
  123.6 79.8 %copy-start.50 = (f32[768]{0:T(1024)S(1)}, f32[768]{0:T(1024)}, u32[]{:S(2)}) copy-start(f32[768]{0:T(1024)} %param.33) | copy-start | bytes 9220
  125.3 164.0 %all-reduce.12.cloned.1.call-start = ((), (), s32[]{:S(2)}) async-start(), calls=%async_computation.1 | async-start | bytes 3489792 | tf_op jit(solution)/shard_map/psum | solution.py:156
  214.8 74.5 %copy-start.51 = (f32[768]{0:T(1024)S(1)}, f32[768]{0:T(1024)}, u32[]{:S(2)}) copy-start(f32[768]{0:T(1024)} %param.39) | copy-start | bytes 9220
  214.9 162.9 %all-reduce.14.cloned.1.call-start = ((), (), s32[]{:S(2)}) async-start(), calls=%async_computation.2 | async-start | bytes 3489792 | tf_op jit(solution)/shard_map/psum | solution.py:149
  303.4 160.2 %all-reduce.16.cloned.1.call-start = ((), (), s32[]{:S(2)}) async-start(), calls=%async_computation.3 | async-start | bytes 3489792 | tf_op jit(solution)/shard_map/psum | solution.py:156
  380.1 7.0 copy-start.26
  389.2 162.0 %all-reduce.18.cloned.1.call-start = ((), (), s32[]{:S(2)}) async-start(), calls=%async_computation.4 | async-start | bytes 3489792 | tf_op jit(solution)/shard_map/psum | solution.py:241
  476.7 166.9 %all-reduce.20.cloned.1.call-start = ((), (), s32[]{:S(2)}) async-start(), calls=%async_computation.5 | async-start | bytes 3489792 | tf_op jit(solution)/shard_map/psum | solution.py:316
  551.2 5.4 slice-start
  565.2 192.7 %all-reduce.22.cloned.1.call-start = ((), (), s32[]{:S(2)}) async-start(), calls=%async_computation.6 | async-start | bytes 14155776 | tf_op jit(solution)/shard_map/psum | solution.py:336
  580.0 8.8 %copy-start.38 = (s32[561,561]{0,1:T(8,128)S(1)}, s32[561,561]{0,1:T(8,128)}, u32[]{:S(2)}) copy-start(s32[561,561]{0,1:T(8,128)} %copy-done.37) | copy-start | bytes 3776656
  588.9 14.7 %copy-start.36 = (s32[561,561]{0,1:T(8,128)S(1)}, s32[561,561]{0,1:T(8,128)}, u32[]{:S(2)}) copy-start(s32[561,561]{0,1:T(8,128)} %copy-done.35) | copy-start | bytes 3776656
  603.5 14.9 %copy-start.53 = (f32[768]{0:T(1024)S(1)}, f32[768]{0:T(1024)}, u32[]{:S(2)}) copy-start(f32[768]{0:T(1024)} %get-tuple-element.74) | copy-start | bytes 9220
  603.5 14.9 %copy-start.54 = (f32[768]{0:T(1024)S(1)}, f32[768]{0:T(1024)}, u32[]{:S(2)}) copy-start(f32[768]{0:T(1024)} %get-tuple-element.96) | copy-start | bytes 9220
  603.5 14.9 %copy-start.58 = (f32[768]{0:T(1024)S(1)}, f32[768]{0:T(1024)}, u32[]{:S(2)}) copy-start(f32[768]{0:T(1024)} %get-tuple-element.124) | copy-start | bytes 9220
  (51 other events, 104.3 us)
Sparse Core Ops, SparseCore 0:
  125.4 77.9 all-reduce.9
  215.0 74.2 all-reduce.11
  303.5 74.2 all-reduce.13
  389.3 74.2 all-reduce.15
  476.9 74.2 all-reduce.17
  565.3 74.2 all-reduce.19
  644.8 112.9 all-reduce.21
where the time goes:
time: 779 us; the launch traced here: 775 us
  waiting for transfers between devices  486 us (62%)
  matrix products  166 us (21%)
  other arithmetic  54.1 us (7%)
  local copies, waits for them, and re-layouts  27.4 us (4%)
  blocking collectives  25.3 us (3%)
  between operations  15.1 us (2%)
    psum x2, waiting for transfers between devices, forward(): branch = lax.psum(partial_value, 'narrow') + b_out  152 us
    psum x2, waiting for transfers between devices, forward(): residual_two = hidden + (lax.psum(ff_part, 'narrow') + b_down)  149 us
    psum x1, waiting for transfers between devices, local(): lax.psum((grad_w_query, grad_b_query, grad_w_key, grad_w_value, grad_b_va...  111 us
    psum x1, waiting for transfers between devices, local(): grad_hidden = grad_residual_two + lax.psum(hidden_part, 'narrow')  74.3 us
    dot_general x3, matrix products, relative_one_page(): jnp.einsum('hb,qkb->hqk', table, chooser, precision=HIGHEST, preferred_el...  73.4 us
    dot_general x3, matrix products, table_one_page(): jnp.einsum('hqk,qkb->hb', grad_page, one_hot_of(grid, bins, jnp.bfloat16)...  38.3 us
    unnamed x142, local copies, waits for them, and re-layouts  26.4 us
    psum x1, blocking collectives, local(): lax.psum((grad_w_query, grad_b_query, grad_w_key, grad_w_value, grad_b_va...  25.3 us
  transfers between devices with their start and end apart: 7, of which 6 were waited for; matrix products, arithmetic and copies ran while one was open for 7% of the time, Pallas kernels for 0%

commit v1 on v0

--- a/solution.py
+++ b/solution.py
@@ -238,7 +238,7 @@
     grad_b_in = jnp.sum(grad_pre, axis=0, dtype=jnp.float32)
     grad_w_in = jnp.einsum("td,tf->df", hidden_low, grad_pre, preferred_element_type=jnp.float32)
     hidden_part = jnp.einsum("tf,df->td", grad_pre, in_weight, preferred_element_type=jnp.float32)
-    grad_hidden = grad_residual_two + lax.psum(hidden_part, "narrow")
+    grad_hidden = grad_residual_two + jnp.sum(lax.all_gather(hidden_part, "narrow"), axis=0)
     _, first_back = jax.vjp(norm_layer, residual_one, ln1_gain, ln1_bias)
     grad_residual_one, grad_ln1_gain, grad_ln1_bias = first_back(grad_hidden)
     grad_branch = grad_residual_one.astype(jnp.bfloat16)

time: 779 us -> 840 us (1.078)
  waiting for transfers between devices: 486 us -> 535 us
    all_gather x0 -> x1, waiting for transfers between devices: none -> 126 us  [local(): lax.all_gather(hidden_part, 'narrow')]
    psum x1 -> x0, waiting for transfers between devices: 74.3 us -> none  [local(): grad_hidden = grad_residual_two + lax.psum(hidden_part, 'narrow')]
    unnamed x142 -> x158, local copies, waits for them, and re-layouts: 26.4 us -> 27.1 us
where the time goes in v1:
time: 840 us; the launch traced here: 831 us
  waiting for transfers between devices  535 us (64%)
  matrix products  166 us (20%)
  other arithmetic  58.8 us (7%)
  local copies, waits for them, and re-layouts  28 us (3%)
  blocking collectives  26.4 us (3%)
  between operations  15.4 us (2%)
    psum x2, waiting for transfers between devices, forward(): branch = lax.psum(partial_value, 'narrow') + b_out  152 us
    psum x2, waiting for transfers between devices, forward(): residual_two = hidden + (lax.psum(ff_part, 'narrow') + b_down)  148 us
    all_gather x1, waiting for transfers between devices, local(): lax.all_gather(hidden_part, 'narrow')  126 us
    psum x1, waiting for transfers between devices, local(): lax.psum((grad_w_query, grad_b_query, grad_w_key, grad_w_value, grad_b_va...  109 us
    dot_general x3, matrix products, relative_one_page(): jnp.einsum('hb,qkb->hqk', table, chooser, precision=HIGHEST, preferred_el...  73.7 us
    dot_general x3, matrix products, table_one_page(): jnp.einsum('hqk,qkb->hb', grad_page, one_hot_of(grid, bins, jnp.bfloat16)...  38.4 us
    unnamed x158, local copies, waits for them, and re-layouts  27.1 us
    psum x1, blocking collectives, local(): lax.psum((grad_w_query, grad_b_query, grad_w_key, grad_w_value, grad_b_va...  26.4 us
  transfers between devices with their start and end apart: 7, of which 6 were waited for; matrix products, arithmetic and copies ran while one was open for 7% of the time, Pallas kernels for 0%

profile of v1, /device:TPU:0, one launch (start us, length us, event | category | flops | bytes accessed | tf_op | source)
XLA Modules:
  0.0 830.7 jit_solution(16110903949797491050)
XLA Ops:
  7.3 12.5 %fusion.117 = s32[561]{0:T(1024)S(1)} fusion(s32[561]{0:T(1024)} %param.24), kind=kLoop, calls=%fused_computation.186 | loop fusion | flops 943602 | bytes 4488 | tf_op jit(solution)/shard_map/reduce_sum | solution.py:60
  23.8 14.3 %fusion.10 = f32[561,561,3]{0,2,1:T(4,128)S(1)} fusion(s32[561,561]{0,1:T(8,128)S(1)} %convert_add_fusion.2, f32[3,32]{1,0:T(4,128)S(1)} %copy-done), kind=kOutput, calls=%fused_computation.13 | convolution fusion | flops 372629664 | bytes 5035920 | tf_op jit(solution)/shard_map/while/body/eval_jaxpr/hb,qkb->hqk/dot_general | solution.py:81
  38.1 9.3 %convert_add_fusion = (s32[561,561]{0,1:T(8,128)S(1)}, s32[561,561]{0,1:T(8,128)S(1)}) fusion(s32[561]{0:T(1024)S(1)} %get-tuple-element.77, s32[561]{0:T(1024)S(1)} %get-tuple-element.76), kind=kLoop, calls=%fused_computation.183 | loop fusion | flops 61055736 | bytes 2522256 | tf_op jit(solution)/shard_map/while/body/eval_jaxpr/add | solution.py:43
  47.5 29.7 %fusion.2 = f32[561,561,3]{0,2,1:T(4,128)} fusion(s32[561,561]{0,1:T(8,128)S(1)} %get-tuple-element.126, f32[3,64]{1,0:T(4,128)S(1)} %copy-done.68), kind=kOutput, calls=%fused_computation.3 | convolution fusion | flops 745259328 | bytes 5036304 | tf_op jit(solution)/shard_map/while/body/eval_jaxpr/hb,qkb->hqk/dot_general | solution.py:81
  77.3 29.7 %fusion.4 = f32[561,561,3]{0,2,1:T(4,128)} fusion(s32[561,561]{0,1:T(8,128)S(1)} %get-tuple-element.127, f32[3,64]{1,0:T(4,128)S(1)} %copy-done.69), kind=kOutput, calls=%fused_computation.6 | convolution fusion | flops 745259328 | bytes 5036304 | tf_op jit(solution)/shard_map/while/body/eval_jaxpr/hb,qkb->hqk/dot_general | solution.py:81
  108.6 5.0 fusion.13
  118.2 4.8 fusion.121
  124.8 78.0 %all-reduce.9.cloned.1.call-done = f32[561,768]{1,0:T(8,128)} async-done(((f32[561,768]{1,0:T(8,128)}), f32[561,768]{1,0:T(8,128)}) %all-reduce.9.cloned.1.call-update) | async-done | bytes 1723408 | tf_op jit(solution)/shard_map/psum | solution.py:149
  205.4 8.9 %fusion.120 = f32[561,768]{1,0:T(8,128)} fusion(f32[561,768]{1,0:T(8,128)S(1)} %get-tuple-element.114, f32[768]{0:T(1024)S(1)} %copy-done.67, f32[768]{0:T(1024)S(1)} %copy-done.59, f32[768]{0:T(1024)S(1)} %copy-done.55, f32[561]{0:T(1024)S(1)} %add_rsqrt_fusion.1, f32[561]{0:T(1024)S(1)} %broadcast_multiply_fusion.3, f32[768,768]{1,0:T(8,128)} %param.38, ...), kind=kOutput, calls=%fused_computation.195 | convolution fusion | flops 1355334912 | bytes 8179080 | tf_op jit(solution)/shard_map/dot_general | solution.py:155
  214.8 74.0 %all-reduce.11.cloned.1.call-done = f32[561,768]{1,0:T(8,128)} async-done(((f32[561,768]{1,0:T(8,128)}), f32[561,768]{1,0:T(8,128)}) %all-reduce.11.cloned.1.call-update) | async-done | bytes 1723408 | tf_op jit(solution)/shard_map/psum | solution.py:156
  302.9 74.4 %all-reduce.13.cloned.1.call-done = f32[561,768]{1,0:T(8,128)} async-done(((f32[561,768]{1,0:T(8,128)}), f32[561,768]{1,0:T(8,128)}) %all-reduce.13.cloned.1.call-update) | async-done | bytes 1723408 | tf_op jit(solution)/shard_map/psum | solution.py:149
  379.6 6.0 multiply_convert_fusion.1
  388.8 74.2 %all-reduce.15.cloned.1.call-done = f32[561,768]{1,0:T(8,128)} async-done(((f32[561,768]{1,0:T(8,128)}), f32[561,768]{1,0:T(8,128)}) %all-reduce.15.cloned.1.call-update) | async-done | bytes 1723408 | tf_op jit(solution)/shard_map/psum | solution.py:156
  476.3 125.7 %all-gather.4.cloned.1.call-done = f32[4,561,768]{2,1,0:T(8,128)} async-done(((f32[1,561,768]{2,1,0:T(8,128)}), f32[4,561,768]{2,1,0:T(8,128)}) %all-gather.4.cloned.1.call-update) | async-done | bytes 6893584 | tf_op jit(solution)/shard_map/all_gather | solution.py:241
  602.0 4.8 reduce_sum.258
  606.8 3.2 multiply_reduce_fusion.2
  622.5 3.8 fusion.264
  626.3 2.9 fusion.248
  636.8 8.8 %fusion.132 = f32[3,32]{1,0:T(4,128)S(1)} fusion(s32[561,561]{0,1:T(8,128)} %copy-done.39, bf16[3,561,561]{1,2,0:T(8,128)(2,1)S(1)} %copy-done.8), kind=kOutput, calls=%fused_computation.208 | convolution fusion | flops 70497504 | bytes 3147594 | tf_op jit(solution)/shard_map/while/body/eval_jaxpr/hqk,qkb->hb/dot_general | solution.py:97
  645.7 14.6 %fusion.135 = f32[3,64]{1,0:T(4,128)S(1)} fusion(s32[561,561]{0,1:T(8,128)S(1)} %copy-done.43, bf16[3,561,561]{1,2,0:T(8,128)(2,1)S(1)} %copy-done.8), kind=kOutput, calls=%fused_computation.209 | convolution fusion | flops 140995008 | bytes 3147978 | tf_op jit(solution)/shard_map/while/body/eval_jaxpr/hqk,qkb->hb/dot_general | solution.py:97
  660.4 14.9 %fusion.138 = f32[3,64]{1,0:T(4,128)S(1)} fusion(s32[561,561]{0,1:T(8,128)S(1)} %copy-done.41, bf16[3,561,561]{1,2,0:T(8,128)(2,1)S(1)} %copy-done.8), kind=kOutput, calls=%fused_computation.210 | convolution fusion | flops 140995008 | bytes 3147978 | tf_op jit(solution)/shard_map/while/body/eval_jaxpr/hqk,qkb->hb/dot_general | solution.py:97
  675.3 26.4 %all-reduce = (f32[192]{0:T(256)}, f32[192]{0:T(256)}, f32[768]{0:T(1024)}, f32[768]{0:T(1024)}, f32[768]{0:T(1024)}, /*index=5*/f32[768]{0:T(1024)}, f32[768]{0...) all-reduce(f32[192]{0:T(256)S(1)} %reduce_sum.266, ...), channel_id=1, replica_groups=mesh['wide'=8,'narrow'=4] {'wide'}, use_global_device_ids=true, to_apply=%region_26.27 | all-reduce | flops 6240 | bytes 49920 | tf_op jit(solution)/shard_map/psum | solution.py:336
  701.7 3.4 add_add_fusion.7
  705.1 108.6 %all-reduce.19.cloned.1.call-done = (f32[768,192]{0,1:T(8,128)}, f32[768,192]{0,1:T(8,128)}, f32[768,192]{0,1:T(8,128)}, f32[192,768]{1,0:T(8,128)}, f32[768,768]{1,0:T(8,128)}, /*index=5*/f32[768,768]{1,0:T(8,128)}) async-done(((f32[768,192]{0,1:T(8,128)}, f32[768,192]{0,1:T(8,128)}, f32[768,192]{0,1:T(8,128)}, f32[192,768]{1,0:T(8,128)}, f32[768,768]{1,0:T(8,128)}, /*index=5*/f32[768,768]{1,0:T(8,128)}), ...) | async-done | bytes 7077904 | tf_op jit(solution)/shard_map/psum | solution.py:336
  (237 shorter events, 77.0 us)
Async XLA Ops:
  7.2 16.6 %copy-start = (f32[3,32]{1,0:T(4,128)S(1)}, f32[3,32]{1,0:T(4,128)}, u32[]{:S(2)}) copy-start(f32[3,32]{1,0:T(4,128)} %param.42) | copy-start | bytes 1156
  7.2 195.7 %all-reduce.9.cloned.1.call-start = ((), (), s32[]{:S(2)}) async-start(), calls=%async_computation | async-start | bytes 3489792 | tf_op jit(solution)/shard_map/psum | solution.py:149
  23.0 15.2 %copy-start.39 = (s32[561,561]{0,1:T(8,128)}, s32[561,561]{0,1:T(8,128)S(1)}, u32[]{:S(2)}) copy-start(s32[561,561]{0,1:T(8,128)S(1)} %convert_add_fusion.2) | copy-start | bytes 3776656
  38.1 9.4 %copy-start.68 = (f32[3,64]{1,0:T(4,128)S(1)}, f32[3,64]{1,0:T(4,128)}, u32[]{:S(2)}) copy-start(f32[3,64]{1,0:T(4,128)} %param.44) | copy-start | bytes 2308
  47.5 29.8 %copy-start.40 = (s32[561,561]{0,1:T(8,128)}, s32[561,561]{0,1:T(8,128)S(1)}, u32[]{:S(2)}) copy-start(s32[561,561]{0,1:T(8,128)S(1)} %get-tuple-element.126) | copy-start | bytes 3776656
  47.5 29.8 %copy-start.42 = (s32[561,561]{0,1:T(8,128)}, s32[561,561]{0,1:T(8,128)S(1)}, u32[]{:S(2)}) copy-start(s32[561,561]{0,1:T(8,128)S(1)} %get-tuple-element.127) | copy-start | bytes 3776656
  47.5 29.8 %copy-start.69 = (f32[3,64]{1,0:T(4,128)S(1)}, f32[3,64]{1,0:T(4,128)}, u32[]{:S(2)}) copy-start(f32[3,64]{1,0:T(4,128)} %param.43) | copy-start | bytes 2308
  77.3 29.7 %copy-start.3 = (f32[561,768]{1,0:T(8,128)S(1)}, f32[561,768]{1,0:T(8,128)}, u32[]{:S(2)}) copy-start(f32[561,768]{1,0:T(8,128)} %param.23) | copy-start | bytes 5170180
  77.3 29.7 %copy-start.15 = (f32[768,192]{0,1:T(8,128)S(1)}, f32[768,192]{0,1:T(8,128)}, u32[]{:S(2)}) copy-start(f32[768,192]{0,1:T(8,128)} %param.29) | copy-start | bytes 1769476
  123.1 79.8 %copy-start.57 = (f32[768]{0:T(1024)S(1)}, f32[768]{0:T(1024)}, u32[]{:S(2)}) copy-start(f32[768]{0:T(1024)} %param.33) | copy-start | bytes 9220
  124.8 164.0 %all-reduce.11.cloned.1.call-start = ((), (), s32[]{:S(2)}) async-start(), calls=%async_computation.1 | async-start | bytes 3489792 | tf_op jit(solution)/shard_map/psum | solution.py:156
  214.3 74.5 %copy-start.58 = (f32[768]{0:T(1024)S(1)}, f32[768]{0:T(1024)}, u32[]{:S(2)}) copy-start(f32[768]{0:T(1024)} %param.39) | copy-start | bytes 9220
  214.3 163.0 %all-reduce.13.cloned.1.call-start = ((), (), s32[]{:S(2)}) async-start(), calls=%async_computation.2 | async-start | bytes 3489792 | tf_op jit(solution)/shard_map/psum | solution.py:149
  302.9 160.2 %all-reduce.15.cloned.1.call-start = ((), (), s32[]{:S(2)}) async-start(), calls=%async_computation.3 | async-start | bytes 3489792 | tf_op jit(solution)/shard_map/psum | solution.py:156
  379.6 6.9 copy-start.26
  388.6 213.4 %all-gather.4.cloned.1.call-start = ((), (), s32[]{:S(2)}) async-start(), calls=%async_computation.5 | async-start | bytes 8724480 | tf_op jit(solution)/shard_map/all_gather | solution.py:241
  476.2 225.5 %all-reduce.17.cloned.1.call-start = ((), (), s32[]{:S(2)}) async-start(), calls=%async_computation.4 | async-start | bytes 3489792 | tf_op jit(solution)/shard_map/psum | solution.py:316
  621.4 192.4 %all-reduce.19.cloned.1.call-start = ((), (), s32[]{:S(2)}) async-start(), calls=%async_computation.6 | async-start | bytes 14155776 | tf_op jit(solution)/shard_map/psum | solution.py:336
  636.8 8.8 %copy-start.43 = (s32[561,561]{0,1:T(8,128)S(1)}, s32[561,561]{0,1:T(8,128)}, u32[]{:S(2)}) copy-start(s32[561,561]{0,1:T(8,128)} %copy-done.42) | copy-start | bytes 3776656
  645.7 14.7 %copy-start.41 = (s32[561,561]{0,1:T(8,128)S(1)}, s32[561,561]{0,1:T(8,128)}, u32[]{:S(2)}) copy-start(s32[561,561]{0,1:T(8,128)} %copy-done.40) | copy-start | bytes 3776656
  660.3 14.9 %copy-start.60 = (f32[768]{0:T(1024)S(1)}, f32[768]{0:T(1024)}, u32[]{:S(2)}) copy-start(f32[768]{0:T(1024)} %get-tuple-element.74) | copy-start | bytes 9220
  660.3 14.9 %copy-start.61 = (f32[768]{0:T(1024)S(1)}, f32[768]{0:T(1024)}, u32[]{:S(2)}) copy-start(f32[768]{0:T(1024)} %get-tuple-element.96) | copy-start | bytes 9220
  660.3 14.9 %copy-start.62 = (f32[768]{0:T(1024)S(1)}, f32[768]{0:T(1024)}, u32[]{:S(2)}) copy-start(f32[768]{0:T(1024)} %get-tuple-element.75) | copy-start | bytes 9220
  660.3 14.9 %copy-start.66 = (f32[768]{0:T(1024)S(1)}, f32[768]{0:T(1024)}, u32[]{:S(2)}) copy-start(f32[768]{0:T(1024)} %get-tuple-element.124) | copy-start | bytes 9220
  (59 other events, 126.0 us)
Sparse Core Ops, SparseCore 0:
  124.9 77.9 all-reduce.8
  214.4 74.2 all-reduce.10
  303.0 74.2 all-reduce.12
  388.7 74.2 all-reduce.14
  476.3 125.6 all-gather.3
  621.5 73.4 all-reduce.16
  700.8 112.9 all-reduce.18
